TPU v7x, 256 devices: a whole 4x4x8 slice. The times are simulated.
256 devices in a mesh: state: 32 (over z_lo, y, core), det: 8 (over x, z_hi).
Axes of the slice: x: 4, y: 4, z: 8 (z_hi: 2, z_lo: 4; z = z_hi * 4 + z_lo), core: 2. Of those that a mesh axis runs over, the one named last changes fastest.
Arguments:
- amplitudes: bfloat16 [128, 16384, 324], P('state', 'det'), may hold values from -0.046875 to 0.046875
Outputs:
- density_tiles: float32 [2, 512, 324, 324], P(None, ('state', 'det'))
All inputs are finite; a program needn't handle non-finite values.
Results may differ from a plain program's by a relative error of at most 0.0003.
Values may be sent and summed in bfloat16 or wider, within the bound.
A program may use at most 128 MiB of HBM per device.

v0:
```python
import jax
import jax.numpy as jnp
from jax import lax
from jax.sharding import PartitionSpec as P


def partner_2(value, axis, stride):
    mask = 2**stride
    pairs = [(source, source ^ mask) for source in range(lax.axis_size(axis))]
    return lax.ppermute(value, axis, pairs)


def pair_terms(own_block, partner, count):
    operators = own_block.shape[2]
    terms = jnp.einsum("adp,bdq->abpq", own_block, partner, preferred_element_type=jnp.float32)
    return terms.reshape(count, operators, operators)


def on_device(amplitudes):
    blocks = lax.axis_size("state")
    far_bit = blocks.bit_length() - 2
    states = amplitudes.shape[0]
    owned = states * states // lax.axis_size("det")
    gathered = []
    for bit in (far_bit, 0):
        partner = partner_2(amplitudes, "state", bit)
        gathered.append(
            lax.psum_scatter(
                pair_terms(amplitudes, partner, owned * lax.axis_size("det")),
                "det",
                scatter_dimension=0,
                tiled=True,
            )
        )
    return jnp.stack(gathered)


def solution(mesh):
    placed = (P("state", "det", None),)
    return jax.shard_map(
        on_device,
        mesh=mesh,
        in_specs=placed,
        out_specs=P(None, ("state", "det"), None, None),
        check_vma=False,
    )
```

profile of v0, /device:TPU:22, one launch (start us, length us, event | category | flops | bytes accessed | tf_op | source)
XLA Modules:
  0.0 643.3 jit_solution(12611833024205811501)
XLA Ops:
  6.5 0.0 reduce-scatter.3.cloned.1.call-start
  6.5 3.3 collective-permute-start
  9.8 228.4 %collective-permute-done = bf16[4,2048,324]{1,0,2:T(4,128)(2,1)S(1)} collective-permute-done((bf16[4,2048,324]{1,0,2:T(4,128)(2,1)}, bf16[4,2048,324]{1,0,2:T(4,128)(2,1)S(1)}, u32[]{:S(2)}, u32[]{:S(2)}) %collective-permute-start) | collective-permute-done | bytes 5308448 | tf_op jit(solution)/shard_map/ppermute | solution.py:10
  238.2 23.9 %fusion.8 = f32[4,4,324,324]{2,3,0,1:T(8,128)} fusion(bf16[4,2048,324]{1,0,2:T(4,128)(2,1)} %param.1, bf16[4,2048,324,1]{1,0,2,3:T(4,128)(2,1)S(1)} %bitcast.24), kind=kOutput, calls=%fused_computation.8 | convolution fusion | flops 6879707136 | bytes 17335296 | tf_op jit(solution)/shard_map/adp,bdq->abpq/dot_general | solution.py:15
  262.1 8.9 %copy.15 = f32[4,4,324,324]{3,2,1,0:T(8,128)} copy(f32[4,4,324,324]{2,3,0,1:T(8,128)} %fusion.8) | data formatting | bytes 13436928 | tf_op jit(solution)/shard_map/adp,bdq->abpq/transpose | solution.py:15
  271.0 0.0 reduce-scatter.3.cloned.1.call-update
  271.0 0.0 reduce-scatter.5.cloned.1.call-start
  271.1 0.3 collective-permute-start.1
  271.4 8.9 %collective-permute-done.1 = bf16[4,2048,324]{1,0,2:T(4,128)(2,1)S(1)} collective-permute-done((bf16[4,2048,324]{1,0,2:T(4,128)(2,1)}, bf16[4,2048,324]{1,0,2:T(4,128)(2,1)S(1)}, u32[]{:S(2)}, u32[]{:S(2)}) %collective-permute-start.1) | collective-permute-done | bytes 5308448 | tf_op jit(solution)/shard_map/ppermute | solution.py:10
  280.3 23.9 %fusion.13 = f32[4,4,324,324]{2,3,0,1:T(8,128)} fusion(bf16[4,2048,324]{1,0,2:T(4,128)(2,1)} %param.1, bf16[4,2048,324,1]{1,0,2,3:T(4,128)(2,1)S(1)} %bitcast.25), kind=kOutput, calls=%fused_computation.9 | convolution fusion | flops 6879707136 | bytes 17335296 | tf_op jit(solution)/shard_map/adp,bdq->abpq/dot_general | solution.py:15
  304.2 8.9 %copy.18 = f32[4,4,324,324]{3,2,1,0:T(8,128)} copy(f32[4,4,324,324]{2,3,0,1:T(8,128)} %fusion.13) | data formatting | bytes 13436928 | tf_op jit(solution)/shard_map/adp,bdq->abpq/transpose | solution.py:15
  313.1 0.0 reduce-scatter.5.cloned.1.call-update
  313.1 139.1 %reduce-scatter.3.cloned.1.call-done = f32[2,324,324]{2,1,0:T(8,128)} async-done(((f32[16,324,324]{2,1,0:T(8,128)}), f32[2,324,324]{2,1,0:T(8,128)}) %reduce-scatter.3.cloned.1.call-update) | async-done | bytes 839824 | tf_op jit(solution)/shard_map/reduce_scatter | solution.py:28
  452.2 180.3 %reduce-scatter.5.cloned.1.call-done = f32[2,324,324]{2,1,0:T(8,128)} async-done(((f32[16,324,324]{2,1,0:T(8,128)}), f32[2,324,324]{2,1,0:T(8,128)}) %reduce-scatter.5.cloned.1.call-update) | async-done | bytes 839824 | tf_op jit(solution)/shard_map/reduce_scatter | solution.py:28
  632.5 1.6 pad_maximum_fusion
  634.1 2.3 copy.19
Async XLA Ops:
  6.5 445.7 %reduce-scatter.3.cloned.1.call-start = ((), (), s32[]{:S(2)}) async-start(), calls=%async_computation.2 | async-start | bytes 9068544 | tf_op jit(solution)/shard_map/reduce_scatter | solution.py:28
  6.5 231.7 %collective-permute-start = (bf16[4,2048,324]{1,0,2:T(4,128)(2,1)}, bf16[4,2048,324]{1,0,2:T(4,128)(2,1)S(1)}, u32[]{:S(2)}, u32[]{:S(2)}) collective-permute-start(bf16[4,2048,324]{1,0,2:T(4,128)(2,1)} %param.1), channel_id=1, source_target_pairs={{0,128},{8,136},{16,144},{24,152},{32,160},{40,168},{48,176},{56,1... | collective-permute-start | bytes 15925256 | tf_op jit(solution)/shard_map/ppermute | solution.py:10
  271.0 361.5 %reduce-scatter.5.cloned.1.call-start = ((), (), s32[]{:S(2)}) async-start(), calls=%async_computation.3 | async-start | bytes 9068544 | tf_op jit(solution)/shard_map/reduce_scatter | solution.py:28
  271.1 9.2 %collective-permute-start.1 = (bf16[4,2048,324]{1,0,2:T(4,128)(2,1)}, bf16[4,2048,324]{1,0,2:T(4,128)(2,1)S(1)}, u32[]{:S(2)}, u32[]{:S(2)}) collective-permute-start(bf16[4,2048,324]{1,0,2:T(4,128)(2,1)} %param.1), channel_id=1, source_target_pairs={{0,8},{8,0},{16,24},{24,16},{32,40},{40,32},{48,56},{56,48},{64,72... | collective-permute-start | bytes 15925256 | tf_op jit(solution)/shard_map/ppermute | solution.py:10
Sparse Core Ops, SparseCore 0:
  271.1 181.0 reduce-scatter.2
  456.5 175.9 reduce-scatter.4
where the time goes:
time: 645 us; the launch traced here: 643 us
  waiting for transfers between devices  557 us (86%)
  matrix products  47.8 us (7%)
  local copies, waits for them, and re-layouts  20 us (3%)
  between operations  13.4 us (2%)
    reduce_scatter x2, waiting for transfers between devices, on_device(): lax.psum_scatter(pair_terms(amplitudes, partner, owned * lax.axis_size('d...  319 us
    ppermute x2, waiting for transfers between devices, partner_2(): return lax.ppermute(value, axis, pairs)  237 us
    dot_general x2, matrix products, pair_terms(): jnp.einsum('adp,bdq->abpq', own_block, partner, preferred_element_type=jn...  47.8 us
    transpose x2, local copies, waits for them, and re-layouts, pair_terms(): jnp.einsum('adp,bdq->abpq', own_block, partner, preferred_element_type=jn...  17.7 us
  transfers between devices with their start and end apart: 4, of which 4 were waited for; matrix products, arithmetic and copies ran while one was open for 5% of the time, Pallas kernels for 0%

commit v1 on v0

v1 whole, which is shorter than its diff:
```python
import functools

import jax
import jax.numpy as jnp
from jax import lax
from jax.experimental import pallas as pl
from jax.experimental.pallas import tpu as pltpu
from jax.sharding import Mesh, PartitionSpec as P

MESH = pl.DeviceIdType.MESH
ROWS = 336
CHUNK = 112
CHUNKS = 3
HALF = 168
FAR = 2 * CHUNKS


def group_of(a, scheme):
    if scheme == 0:
        return ((a + 1) // 2) % 2, a // 2
    return a // 2, a % 2


def product(left, right):
    return lax.dot_general(left, right, (((1,), (1,)), ((), ())), preferred_element_type=jnp.float32)


class Stream:
    def __init__(self, refs, index, sems, first_sem, scheme, mirror):
        self.t, self.r1, self.r2, self.r3, self.f, self.r4 = (ref.at[index] for ref in refs)
        self.send_sem, self.recv_sem = sems
        self.sem = first_sem
        x, self.zh = lax.axis_index("x"), lax.axis_index("zh")
        self.group, self.member = group_of(x, scheme)
        near, far = {"x": x + 1 - 2 * (x % 2)}, {"x": 3 - x}
        self.partners = (near, far) if scheme == 0 else (far, near)
        self.partners = self.partners + ({"zh": 1 - self.zh}, mirror)

    def copy(self, step):
        source, target = (
            (self.t.at[1 - self.group], self.r1),
            (self.t.at[self.group, 1 - self.member], self.r2),
            (self.t.at[self.group, self.member, 1 - self.zh], self.r3),
            (self.f, self.r4),
        )[step]
        return pltpu.make_async_remote_copy(
            src_ref=source,
            dst_ref=target,
            send_sem=self.send_sem.at[self.sem + step],
            recv_sem=self.recv_sem.at[self.sem + step],
            device_id=self.partners[step],
            device_id_type=MESH,
        )

    def over_x(self):
        self.copy(0).start()

    def over_x_again(self):
        self.copy(0).wait_recv()
        g, m = self.group, self.member
        self.t[g, 1 - m] += self.r1[1 - m]
        self.copy(1).start()
        self.t[g, m] += self.r1[m]

    def over_zh(self):
        self.copy(1).wait_recv()
        g, m, h = self.group, self.member, self.zh
        self.t[g, m, 1 - h] += self.r2[1 - h]
        self.copy(2).start()
        self.t[g, m, h] += self.r2[h]

    def to_mirror(self):
        self.copy(2).wait_recv()
        self.f[...] = self.t[self.group, self.member, self.zh] + self.r3[...]
        self.copy(3).start()

    def finish(self):
        self.copy(3).wait_recv()

    def drain(self):
        for step in range(4):
            self.copy(step).wait_send()


def kernel(
    a_ref, out_ref, own, beside, held,
    t0, r10, r20, r30, f0, r40, t1, r11, r21, r31, f1, r41,
    send_sem, recv_sem, load_sem, ex_send, ex_recv,
):
    zb, core = lax.axis_index("zb"), lax.axis_index("core")
    x, zh = lax.axis_index("x"), lax.axis_index("zh")
    half = own.shape[2] // 2

    def mirror(s, side, name):
        b = 2 * zh + (x + s) % 2
        return {name: 1 - side, "x": b, "zh": x // 2}

    far_mirrors = [mirror(s, zb, "zb") for s in range(2)]
    near_mirror = mirror(core, core, "core")
    partners = [
        {"zb": 1 - zb}, {"core": 1 - core}, {"x": x + 1 - 2 * (x % 2)}, {"x": 3 - x}, {"zh": 1 - zh},
        *far_mirrors, near_mirror,
    ]
    barrier = pltpu.get_barrier_semaphore()
    for partner in partners:
        pl.semaphore_signal(barrier, inc=1, device_id=partner, device_id_type=MESH)
    pl.semaphore_wait(barrier, len(partners))

    here = pl.ds(pl.multiple_of(zb * half, half), half)
    away = pl.ds(pl.multiple_of((1 - zb) * half, half), half)
    load = pltpu.make_async_copy(a_ref, own, load_sem)
    load.start()
    to_side = pltpu.make_async_remote_copy(
        src_ref=a_ref, dst_ref=beside, send_sem=ex_send.at[CHUNKS], recv_sem=ex_recv.at[CHUNKS],
        device_id={"core": 1 - core}, device_id_type=MESH,
    )
    exchange = []
    for c in range(CHUNKS):
        rows = pl.ds(c * CHUNK, CHUNK)
        exchange.append(pltpu.make_async_remote_copy(
            src_ref=a_ref.at[:, rows, away], dst_ref=held.at[:, rows, :],
            send_sem=ex_send.at[c], recv_sem=ex_recv.at[c],
            device_id={"zb": 1 - zb}, device_id_type=MESH,
        ))
    exchange[0].start()
    to_side.start()
    for copy in exchange[1:]:
        copy.start()

    sems = (send_sem, recv_sem)
    far = [
        [
            Stream((t0, r10, r20, r30, f0, r40), 2 * c + s, sems, 4 * (2 * c + s), s, far_mirrors[s])
            for s in range(2)
        ]
        for c in range(CHUNKS)
    ]
    near = [
        Stream((t1, r11, r21, r31, f1, r41), h, sems, 4 * (FAR + h), h, near_mirror) for h in range(2)
    ]

    load.wait()
    to_side.wait_recv()

    @pl.loop(0, 4)
    def _(a):
        parity = (a + core) % 2
        for bh in range(2):
            tile = product(beside[2 * bh + parity], own[a])
            for h in range(2):
                g, m = group_of(a, h)
                t1[h, g, m, bh] = tile[h * HALF:(h + 1) * HALF]

    for stream in near:
        stream.over_x()
    for stream in near:
        stream.over_x_again()

    def multiply(c):
        exchange[c].wait_recv()
        rows = pl.ds(c * CHUNK, CHUNK)

        @pl.loop(0, 4)
        def _(a):
            left = [held[2 * bh + (a + s) % 2, rows, :] for s in range(2) for bh in range(2)]
            tile = product(jnp.concatenate(left, 0), own[a, :, here])
            for s in range(2):
                g, m = group_of(a, s)
                for bh in range(2):
                    at = (2 * s + bh) * CHUNK
                    t0[2 * c + s, g, m, bh] = tile[at:at + CHUNK]

        for stream in far[c]:
            stream.over_x()

    multiply(0)
    for stream in near:
        stream.over_zh()
    for stream in far[0]:
        stream.over_x_again()
    for stream in far[0]:
        stream.over_zh()
    multiply(1)
    for stream in far[1]:
        stream.over_x_again()
    for stream in far[1]:
        stream.over_zh()
    multiply(2)
    for stream in near:
        stream.to_mirror()
    for stream in far[0]:
        stream.to_mirror()
    for stream in far[2]:
        stream.over_x_again()
    for stream in far[2]:
        stream.over_zh()
    for stream in far[1]:
        stream.to_mirror()

    ops = out_ref.shape[2]
    slot = (x + core) % 2
    for h in range(2):
        near[h].finish()
    tile = jnp.concatenate([f1[0], f1[1]], 0).T
    out_ref[1, slot] = tile[:ops, :ops]
    out_ref[1, 1 - slot] = jnp.concatenate([r41[0], r41[1]], 0)[:ops, :ops]
    for stream in far[2]:
        stream.to_mirror()
    for s in range(2):
        for c in range(CHUNKS):
            far[c][s].finish()
        slot = (x + s) % 2
        tile = jnp.concatenate([f0[2 * c + s] for c in range(CHUNKS)], 0).T
        got = jnp.concatenate([r40[2 * c + s] for c in range(CHUNKS)], 0)
        out_ref[0, slot] = tile[:ops, :ops] + got[:ops, :ops]

    to_side.wait_send()
    for copy in exchange:
        copy.wait_send()
    for streams in (*far, near):
        for stream in streams:
            stream.drain()


def buffers(streams, rows):
    lead = [(2, 2, 2), (2, 2), (2,), (), (), ()]
    return [pltpu.VMEM((streams, *shape, rows, ROWS), jnp.float32) for shape in lead]


def on_device(amplitudes):
    states, dets, ops = amplitudes.shape
    block = jnp.pad(amplitudes.transpose(0, 2, 1), ((0, 0), (0, ROWS - ops), (0, 0)))
    dma = pltpu.SemaphoreType.DMA
    return pl.pallas_call(
        kernel,
        out_shape=jax.ShapeDtypeStruct((2, 2, ops, ops), jnp.float32),
        in_specs=[pl.BlockSpec(memory_space=pl.ANY)],
        out_specs=pl.BlockSpec(memory_space=pltpu.VMEM),
        scratch_shapes=[
            pltpu.VMEM((states, ROWS, dets), jnp.bfloat16),
            pltpu.VMEM((states, ROWS, dets), jnp.bfloat16),
            pltpu.VMEM((states, ROWS, dets // 2), jnp.bfloat16),
            *buffers(FAR, CHUNK),
            *buffers(2, HALF),
            dma((4 * (FAR + 2),)),
            dma((4 * (FAR + 2),)),
            dma,
            dma((CHUNKS + 1,)),
            dma((CHUNKS + 1,)),
        ],
        compiler_params=pltpu.CompilerParams(
            collective_id=0, has_side_effects=True, vmem_limit_bytes=64 * 1024 * 1024 - 65536,
        ),
    )(block)


def solution(mesh):
    fine = Mesh(mesh.devices.reshape(2, 2, 4, 2, 4, 2), ("zb", "za", "y", "core", "x", "zh"))
    state, det = ("zb", "za", "y", "core"), ("x", "zh")
    return jax.shard_map(
        on_device,
        mesh=fine,
        in_specs=(P(state, det, None),),
        out_specs=P(None, state + det, None, None),
        check_vma=False,
    )
```

time: 645 us -> 280 us (0.43)
  waiting for transfers between devices: 557 us -> 0 us
  Pallas kernels: 0 us -> 263 us
  matrix products: 47.8 us -> 0 us
  between operations: 13.4 us -> 0.01 us
  local copies, waits for them, and re-layouts: 20 us -> 12.4 us
    reduce_scatter x2 -> x0, waiting for transfers between devices: 319 us -> none  [on_device(): lax.psum_scatter(pair_terms(amplitudes, partner, owned * lax.axis_size('d...]
    pallas_call x0 -> x1, Pallas kernels: none -> 263 us  [on_device(): pl.pallas_call(kernel, out_shape=jax.ShapeDtypeStruct((2, 2, ops, ops), j...]
    ppermute x2 -> x0, waiting for transfers between devices: 237 us -> none  [partner_2(): return lax.ppermute(value, axis, pairs)]
    dot_general x2 -> x0, matrix products: 47.8 us -> none  [pair_terms(): jnp.einsum('adp,bdq->abpq', own_block, partner, preferred_element_type=jn...]
    transpose x2 -> x0, local copies, waits for them, and re-layouts: 17.7 us -> none  [pair_terms(): jnp.einsum('adp,bdq->abpq', own_block, partner, preferred_element_type=jn...]
  transfers between devices with their start and end apart: 4 -> 0, of which waited for: 4 -> 0; matrix products, arithmetic and copies ran while one was open for 5% -> 0% of each run, Pallas kernels for 0% -> 0%
where the time goes in v1:
time: 280 us; the launch traced here: 275 us
  Pallas kernels  263 us (94%)
  local copies, waits for them, and re-layouts  12.4 us (4%)
    pallas_call x1, Pallas kernels, on_device(): pl.pallas_call(kernel, out_shape=jax.ShapeDtypeStruct((2, 2, ops, ops), j...  263 us

profile of v1, /device:TPU:22, one launch (start us, length us, event | category | flops | bytes accessed | tf_op | source)
XLA Modules:
  0.0 275.3 jit_solution(2018710991308871245)
XLA Ops:
  0.0 5.4 %copy.5 = bf16[4,2048,324]{1,2,0:T(8,128)(2,1)S(1)} copy(bf16[4,2048,324]{1,0,2:T(4,128)(2,1)} %param.1) | data formatting | bytes 10616832 | tf_op args[0]
  5.4 3.1 %pad.4.a_ref = bf16[4,336,2048]{2,1,0:T(8,128)(2,1)} pad(bf16[4,324,2048]{2,1,0:T(8,128)(2,1)S(1)} %bitcast.3, bf16[]{:T(256)} %constant.2.clone.1), padding=0_0x0_12x0_0 | pad | bytes 10813442 | tf_op jit(solution)/shard_map/jit(_pad)/pad | solution.py:232
  8.5 262.9 %shard_map.17 = f32[2,2,324,324]{3,2,1,0:T(8,128)} custom-call(bf16[4,336,2048]{2,1,0:T(8,128)(2,1)} %pad.4.a_ref), custom_call_target="tpu_custom_call" | custom-call | tf_op jit(solution)/shard_map/pallas_call | solution.py:234
  271.5 3.9 %copy.3 = f32[2,2,324,324]{3,1,2,0:T(2,128)} copy(f32[2,2,324,324]{3,2,1,0:T(8,128)} %shard_map.17) | data formatting | bytes 3359232 | tf_op jit(solution)/shard_map/pallas_call | solution.py:234

commit v2 on v0

v2 whole, which is shorter than its diff:
```python
import jax
import jax.numpy as jnp
from jax import lax
from jax.experimental import pallas as pl
from jax.experimental.pallas import tpu as pltpu
from jax.sharding import Mesh, PartitionSpec as P

MESH = pl.DeviceIdType.MESH
ROWS = 336
LANES = 384
CHUNK = 112
CHUNKS = 3
PACKED = 2 * CHUNK + CHUNK // 2 + 8
HOME, AWAY, NEAR = 0, CHUNKS, 2 * CHUNKS
STREAMS = 3 * CHUNKS
STEPS = 4


def group_of(a, scheme):
    if scheme == 0:
        return ((a + 1) // 2) % 2, a // 2
    return a // 2, a % 2


def product(left, right):
    return lax.dot_general(left, right, (((1,), (1,)), ((), ())), preferred_element_type=jnp.float32)


def lanes(rows):
    return lax.broadcasted_iota(jnp.int32, (rows, 128), 1)


def pack(tile):
    third = tile[:, 256:]
    if third.shape[1] < 128:
        third = jnp.concatenate([third, jnp.zeros((CHUNK, 128 - third.shape[1]), jnp.float32)], 1)
    folded = jnp.where(lanes(CHUNK // 2) < 64, third[:CHUNK // 2], pltpu.roll(third[CHUNK // 2:], 64, 1))
    rest = jnp.concatenate([third, jnp.zeros((128 - CHUNK, 128), jnp.float32)], 0).T[64:72]
    return jnp.concatenate([tile[:, :128], tile[:, 128:256], folded, rest], 0)


def unpack(packed):
    folded = packed[2 * CHUNK:PACKED - 8]
    third = jnp.concatenate([folded, pltpu.roll(folded, 64, 1)], 0)
    rest = jnp.concatenate([packed[PACKED - 8:], jnp.zeros((120, 128), jnp.float32)], 0).T[:CHUNK]
    third = jnp.where(lanes(CHUNK) < 64, third, pltpu.roll(rest, 64, 1))
    return jnp.concatenate([packed[:CHUNK], packed[CHUNK:2 * CHUNK], third], 1)


def whole(chunks):
    return jnp.concatenate([unpack(chunk) for chunk in chunks], 0)


def flipped(tile):
    return jnp.concatenate([tile, jnp.zeros((LANES - ROWS, LANES), jnp.float32)], 0).T


def remote(source, target, sends, recvs, send_at, recv_at, device):
    return pltpu.make_async_remote_copy(
        src_ref=source, dst_ref=target, send_sem=sends.at[send_at], recv_sem=recvs.at[recv_at],
        device_id=device, device_id_type=MESH,
    )


class Stream:
    def __init__(self, index, scheme, refs, sems):
        self.t, self.r1, self.r2, self.r3, self.f, self.r4 = (ref.at[index] for ref in refs)
        self.sems, self.sem = sems, STEPS * index
        x, self.zh = lax.axis_index("x"), lax.axis_index("zh")
        self.group, self.member = group_of(x, scheme)
        near, far = {"x": x + 1 - 2 * (x % 2)}, {"x": 3 - x}
        self.first, self.second = (near, far) if scheme == 0 else (far, near)

    def copy(self, step, source, target, device):
        return remote(source, target, *self.sems, self.sem + step, self.sem + step, device)

    def over_x(self):
        self.copy0 = self.copy(0, self.t.at[1 - self.group], self.r1, self.first)
        self.copy0.start()

    def over_x_again(self):
        self.copy0.wait_recv()
        g, m = self.group, self.member
        self.t[g, 1 - m] += self.r1[1 - m]
        self.copy1 = self.copy(1, self.t.at[g, 1 - m], self.r2, self.second)
        self.copy1.start()
        self.t[g, m] += self.r1[m]

    def over_zh(self):
        self.copy1.wait_recv()
        g, m, h = self.group, self.member, self.zh
        self.t[g, m, 1 - h] += self.r2[1 - h]
        self.copy2 = self.copy(2, self.t.at[g, m, 1 - h], self.r3, {"zh": 1 - h})
        self.copy2.start()
        self.t[g, m, h] += self.r2[h]

    def summed(self):
        self.copy2.wait_recv()
        return self.t[self.group, self.member, self.zh] + self.r3[...]

    def to_mirror(self, value, device):
        self.f[...] = value
        self.copy3 = self.copy(3, self.f, self.r4, device)
        self.copy3.start()

    def go_home(self, r5, homes):
        self.copy1.wait_recv()
        g, m = self.group, self.member
        for bh in range(2):
            self.t[g, m, bh] += self.r2[bh]
        self.home_copies = [
            remote(self.t.at[g, m, bh], r5.at[self.zh], *self.sems, self.sem + 2 + bh, self.sem + 2 + self.zh, homes[bh])
            for bh in range(2)
        ]
        for copy in self.home_copies:
            copy.start()
        return [
            remote(self.t.at[g, m, z], r5.at[z], *self.sems, self.sem + 2 + z, self.sem + 2 + z, homes[z])
            for z in range(2)
        ]


def kernel(
    a_ref, out_ref, own, beside, held, t, r1, r2, r3, f, r4, r5,
    send_sem, recv_sem, load_sem, ex_send, ex_recv,
):
    zb, core = lax.axis_index("zb"), lax.axis_index("core")
    x, zh = lax.axis_index("x"), lax.axis_index("zh")
    half = held.shape[2]
    ops, given = out_ref.shape[2], a_ref.shape[1]

    other = {"zb": 1 - zb}
    home_mirror = {**other, "x": 2 * zh + (x + zb) % 2, "zh": x // 2}
    helpers = [{**other, "x": 2 * zh + (x + zb) % 2, "zh": z} for z in range(2)]
    homes = [{**other, "x": 2 * bh + (x + 1 - zb) % 2, "zh": x // 2} for bh in range(2)]
    near_mirror = {"core": 1 - core, "x": 2 * zh + (x + core) % 2, "zh": x // 2}
    partners = [
        other, {"core": 1 - core}, {"x": x + 1 - 2 * (x % 2)}, {"x": 3 - x}, {"zh": 1 - zh},
        *helpers, *homes, near_mirror,
    ]
    barrier = pltpu.get_barrier_semaphore()
    for partner in partners:
        pl.semaphore_signal(barrier, inc=1, device_id=partner, device_id_type=MESH)
    pl.semaphore_wait(barrier, len(partners))

    here = pl.ds(pl.multiple_of(zb * half, half), half)
    away = pl.ds(pl.multiple_of((1 - zb) * half, half), half)
    exchange = []
    for c in range(CHUNKS):
        rows = pl.ds(c * CHUNK, min(CHUNK, given - c * CHUNK))
        exchange.append(
            remote(a_ref.at[:, rows, away], held.at[:, rows, :], ex_send, ex_recv, c, c, other)
        )
        exchange[c].start()
    every = pl.ds(0, given)
    to_side = remote(a_ref, beside.at[:, every, :], ex_send, ex_recv, CHUNKS, CHUNKS, {"core": 1 - core})
    to_side.start()
    load = pltpu.make_async_copy(a_ref, own.at[:, every, :], load_sem)
    load.start()

    refs, sems = (t, r1, r2, r3, f, r4), (send_sem, recv_sem)
    home = [Stream(HOME + c, 0, refs, sems) for c in range(CHUNKS)]
    going = [Stream(AWAY + c, 1, refs, sems) for c in range(CHUNKS)]
    near = [Stream(NEAR + c, c % 2, refs, sems) for c in range(CHUNKS)]

    load.wait()
    to_side.wait_recv()

    @pl.loop(0, 4)
    def _(a):
        for bh in range(2):
            tile = product(beside[2 * bh + (a + core) % 2], own[a])
            for c in range(CHUNKS):
                g, m = group_of(a, c % 2)
                t[NEAR + c, g, m, bh] = pack(tile[c * CHUNK:(c + 1) * CHUNK])

    for stream in near:
        stream.over_x()
    for stream in near:
        stream.over_x_again()

    arrivals = []

    def far_chunk(c, between):
        exchange[c].wait_recv()
        rows = pl.ds(c * CHUNK, CHUNK)

        @pl.loop(0, 4)
        def _(a):
            left = [held[2 * bh + (a + role + zb) % 2, rows, :] for role in range(2) for bh in range(2)]
            tile = product(jnp.concatenate(left, 0), own[a, :, here])
            for role in range(2):
                g, m = group_of(a, role)
                for bh in range(2):
                    start = (2 * role + bh) * CHUNK
                    t[role * AWAY + c, g, m, bh] = pack(tile[start:start + CHUNK])

        home[c].over_x()
        going[c].over_x()
        for stream in between:
            stream.over_zh()
        home[c].over_x_again()
        going[c].over_x_again()
        home[c].over_zh()
        arrivals.append(going[c].go_home(r5.at[c], homes))

    far_chunk(0, near)
    far_chunk(1, ())
    far_chunk(2, ())

    for stream in near:
        stream.to_mirror(stream.summed(), near_mirror)
    slot = (x + core) % 2
    out_ref[1, slot] = flipped(whole([stream.f[...] for stream in near]))[:ops, :ops]

    for c in range(CHUNKS):
        for copy in arrivals[c]:
            copy.wait_recv()
    helped = flipped(whole([r5[c, 0] + r5[c, 1] for c in range(CHUNKS)]))
    for c in range(CHUNKS):
        home[c].to_mirror(home[c].summed() + pack(helped[c * CHUNK:(c + 1) * CHUNK]), home_mirror)
    for stream in near:
        stream.copy3.wait_recv()
    out_ref[1, 1 - slot] = whole([stream.r4[...] for stream in near])[:ops, :ops]
    slot = (x + zb) % 2
    out_ref[0, slot] = flipped(whole([stream.f[...] for stream in home]))[:ops, :ops]
    for stream in home:
        stream.copy3.wait_recv()
    out_ref[0, 1 - slot] = whole([stream.r4[...] for stream in home])[:ops, :ops]

    to_side.wait_send()
    for copy in exchange:
        copy.wait_send()
    for stream in (*home, *near):
        for copy in (stream.copy0, stream.copy1, stream.copy2, stream.copy3):
            copy.wait_send()
    for stream in going:
        for copy in (stream.copy0, stream.copy1, *stream.home_copies):
            copy.wait_send()


def on_device(amplitudes):
    states, dets, ops = amplitudes.shape
    block = jnp.pad(amplitudes.transpose(0, 2, 1), ((0, 0), (0, -ops % 8), (0, 0)))
    dma = pltpu.SemaphoreType.DMA

    def tiles(*lead):
        return pltpu.VMEM((*lead, PACKED, 128), jnp.float32)

    return pl.pallas_call(
        kernel,
        out_shape=jax.ShapeDtypeStruct((2, 2, ops, ops), jnp.float32),
        in_specs=[pl.BlockSpec(memory_space=pl.ANY)],
        out_specs=pl.BlockSpec(memory_space=pltpu.VMEM),
        scratch_shapes=[
            pltpu.VMEM((states, ROWS, dets), jnp.bfloat16),
            pltpu.VMEM((states, ROWS, dets), jnp.bfloat16),
            pltpu.VMEM((states, ROWS, dets // 2), jnp.bfloat16),
            tiles(STREAMS, 2, 2, 2),
            tiles(STREAMS, 2, 2),
            tiles(STREAMS, 2),
            tiles(STREAMS),
            tiles(STREAMS),
            tiles(STREAMS),
            tiles(CHUNKS, 2),
            dma((STREAMS * STEPS,)),
            dma((STREAMS * STEPS,)),
            dma,
            dma((CHUNKS + 1,)),
            dma((CHUNKS + 1,)),
        ],
        compiler_params=pltpu.CompilerParams(
            collective_id=0, has_side_effects=True, vmem_limit_bytes=64 * 1024 * 1024 - 65536,
        ),
    )(block)


def solution(mesh):
    fine = Mesh(mesh.devices.reshape(2, 2, 4, 2, 4, 2), ("zb", "za", "y", "core", "x", "zh"))
    state, det = ("zb", "za", "y", "core"), ("x", "zh")
    return jax.shard_map(
        on_device,
        mesh=fine,
        in_specs=(P(state, det, None),),
        out_specs=P(None, state + det, None, None),
        check_vma=False,
    )
```

time: 645 us -> 271 us (0.42)
  waiting for transfers between devices: 557 us -> 0 us
  Pallas kernels: 0 us -> 259 us
  matrix products: 47.8 us -> 0 us
  between operations: 13.4 us -> 0.01 us
  local copies, waits for them, and re-layouts: 20 us -> 12.3 us
    reduce_scatter x2 -> x0, waiting for transfers between devices: 319 us -> none  [on_device(): lax.psum_scatter(pair_terms(amplitudes, partner, owned * lax.axis_size('d...]
    pallas_call x0 -> x1, Pallas kernels: none -> 259 us  [on_device(): pl.pallas_call(kernel, out_shape=jax.ShapeDtypeStruct((2, 2, ops, ops), j...]
    ppermute x2 -> x0, waiting for transfers between devices: 237 us -> none  [partner_2(): return lax.ppermute(value, axis, pairs)]
    dot_general x2 -> x0, matrix products: 47.8 us -> none  [pair_terms(): jnp.einsum('adp,bdq->abpq', own_block, partner, preferred_element_type=jn...]
    transpose x2 -> x0, local copies, waits for them, and re-layouts: 17.7 us -> none  [pair_terms(): jnp.einsum('adp,bdq->abpq', own_block, partner, preferred_element_type=jn...]
  transfers between devices with their start and end apart: 4 -> 0, of which waited for: 4 -> 0; matrix products, arithmetic and copies ran while one was open for 5% -> 0% of each run, Pallas kernels for 0% -> 0%
where the time goes in v2:
time: 271 us
  Pallas kernels  259 us (96%)
  local copies, waits for them, and re-layouts  12.3 us (5%)
    pallas_call x1, Pallas kernels, on_device(): pl.pallas_call(kernel, out_shape=jax.ShapeDtypeStruct((2, 2, ops, ops), j...  259 us

profile of v2, /device:TPU:22, one launch (start us, length us, event | category | flops | bytes accessed | tf_op | source)
XLA Modules:
  0.0 270.9 jit_solution(7041992456630710546)
XLA Ops:
  0.0 5.4 %copy.5 = bf16[4,2048,324]{1,2,0:T(8,128)(2,1)S(1)} copy(bf16[4,2048,324]{1,0,2:T(4,128)(2,1)} %param.1) | data formatting | bytes 10616832 | tf_op args[0]
  5.4 3.0 %pad.4.a_ref = bf16[4,328,2048]{2,1,0:T(8,128)(2,1)} pad(bf16[4,324,2048]{2,1,0:T(8,128)(2,1)S(1)} %bitcast.3, bf16[]{:T(256)} %constant.2.clone.1), padding=0_0x0_4x0_0 | pad | bytes 10682370 | tf_op jit(solution)/shard_map/jit(_pad)/pad | solution.py:244
  8.5 258.6 %shard_map.17 = f32[2,2,324,324]{3,2,1,0:T(8,128)} custom-call(bf16[4,328,2048]{2,1,0:T(8,128)(2,1)} %pad.4.a_ref), custom_call_target="tpu_custom_call" | custom-call | tf_op jit(solution)/shard_map/pallas_call | solution.py:250
  267.1 3.9 %copy.3 = f32[2,2,324,324]{3,1,2,0:T(2,128)} copy(f32[2,2,324,324]{3,2,1,0:T(8,128)} %shard_map.17) | data formatting | bytes 3359232 | tf_op jit(solution)/shard_map/pallas_call | solution.py:250

commit v3 on v2

--- a/solution.py
+++ b/solution.py
@@ -8,9 +8,9 @@
 MESH = pl.DeviceIdType.MESH
 ROWS = 336
 LANES = 384
-CHUNK = 112
-CHUNKS = 3
-PACKED = 2 * CHUNK + CHUNK // 2 + 8
+SIZES = (96, 96, 80, 64)
+STARTS = (0, 96, 192, 272)
+CHUNKS = len(SIZES)
 HOME, AWAY, NEAR = 0, CHUNKS, 2 * CHUNKS
 STREAMS = 3 * CHUNKS
 STEPS = 4
@@ -30,25 +30,30 @@
     return lax.broadcasted_iota(jnp.int32, (rows, 128), 1)
 
 
+def packed_rows(size):
+    return 2 * size + size // 2 + 8
+
+
 def pack(tile):
-    third = tile[:, 256:]
+    size, third = tile.shape[0], tile[:, 256:]
     if third.shape[1] < 128:
-        third = jnp.concatenate([third, jnp.zeros((CHUNK, 128 - third.shape[1]), jnp.float32)], 1)
-    folded = jnp.where(lanes(CHUNK // 2) < 64, third[:CHUNK // 2], pltpu.roll(third[CHUNK // 2:], 64, 1))
-    rest = jnp.concatenate([third, jnp.zeros((128 - CHUNK, 128), jnp.float32)], 0).T[64:72]
+        third = jnp.concatenate([third, jnp.zeros((size, 128 - third.shape[1]), jnp.float32)], 1)
+    folded = jnp.where(lanes(size // 2) < 64, third[:size // 2], pltpu.roll(third[size // 2:], 64, 1))
+    rest = jnp.concatenate([third, jnp.zeros((128 - size, 128), jnp.float32)], 0).T[64:72]
     return jnp.concatenate([tile[:, :128], tile[:, 128:256], folded, rest], 0)
 
 
-def unpack(packed):
-    folded = packed[2 * CHUNK:PACKED - 8]
+def unpack(packed, size):
+    end = packed_rows(size)
+    folded = packed[2 * size:end - 8]
     third = jnp.concatenate([folded, pltpu.roll(folded, 64, 1)], 0)
-    rest = jnp.concatenate([packed[PACKED - 8:], jnp.zeros((120, 128), jnp.float32)], 0).T[:CHUNK]
-    third = jnp.where(lanes(CHUNK) < 64, third, pltpu.roll(rest, 64, 1))
-    return jnp.concatenate([packed[:CHUNK], packed[CHUNK:2 * CHUNK], third], 1)
+    rest = jnp.concatenate([packed[end - 8:], jnp.zeros((120, 128), jnp.float32)], 0).T[:size]
+    third = jnp.where(lanes(size) < 64, third, pltpu.roll(rest, 64, 1))
+    return jnp.concatenate([packed[:size], packed[size:2 * size], third], 1)
 
 
 def whole(chunks):
-    return jnp.concatenate([unpack(chunk) for chunk in chunks], 0)
+    return jnp.concatenate([unpack(chunk, size) for chunk, size in zip(chunks, SIZES)], 0)
 
 
 def flipped(tile):
@@ -64,7 +69,11 @@
 
 class Stream:
     def __init__(self, index, scheme, refs, sems):
-        self.t, self.r1, self.r2, self.r3, self.f, self.r4 = (ref.at[index] for ref in refs)
+        rows = pl.ds(0, packed_rows(SIZES[index % CHUNKS]))
+        t, r1, r2, r3, f, r4 = refs
+        self.t, self.r1 = t.at[index, :, :, :, rows], r1.at[index, :, :, rows]
+        self.r2 = r2.at[index, :, rows]
+        self.r3, self.f, self.r4 = (ref.at[index, rows] for ref in (r3, f, r4))
         self.sems, self.sem = sems, STEPS * index
         x, self.zh = lax.axis_index("x"), lax.axis_index("zh")
         self.group, self.member = group_of(x, scheme)
@@ -131,12 +140,12 @@
 
     other = {"zb": 1 - zb}
     home_mirror = {**other, "x": 2 * zh + (x + zb) % 2, "zh": x // 2}
-    helpers = [{**other, "x": 2 * zh + (x + zb) % 2, "zh": z} for z in range(2)]
-    homes = [{**other, "x": 2 * bh + (x + 1 - zb) % 2, "zh": x // 2} for bh in range(2)]
+    from_mirror = {**other, "x": 2 * zh + (x + 1 - zb) % 2, "zh": x // 2}
+    homes = [{**other, "zh": z} for z in range(2)]
     near_mirror = {"core": 1 - core, "x": 2 * zh + (x + core) % 2, "zh": x // 2}
     partners = [
-        other, {"core": 1 - core}, {"x": x + 1 - 2 * (x % 2)}, {"x": 3 - x}, {"zh": 1 - zh},
-        *helpers, *homes, near_mirror,
+        {"core": 1 - core}, {"x": x + 1 - 2 * (x % 2)}, {"x": 3 - x}, {"zh": 1 - zh},
+        *homes, home_mirror, from_mirror, near_mirror,
     ]
     barrier = pltpu.get_barrier_semaphore()
     for partner in partners:
@@ -147,11 +156,12 @@
     away = pl.ds(pl.multiple_of((1 - zb) * half, half), half)
     exchange = []
     for c in range(CHUNKS):
-        rows = pl.ds(c * CHUNK, min(CHUNK, given - c * CHUNK))
+        rows = pl.ds(STARTS[c], min(SIZES[c], given - STARTS[c]))
         exchange.append(
             remote(a_ref.at[:, rows, away], held.at[:, rows, :], ex_send, ex_recv, c, c, other)
         )
-        exchange[c].start()
+    for copy in exchange[:-1]:
+        copy.start()
     every = pl.ds(0, given)
     to_side = remote(a_ref, beside.at[:, every, :], ex_send, ex_recv, CHUNKS, CHUNKS, {"core": 1 - core})
     to_side.start()
@@ -172,7 +182,7 @@
             tile = product(beside[2 * bh + (a + core) % 2], own[a])
             for c in range(CHUNKS):
                 g, m = group_of(a, c % 2)
-                t[NEAR + c, g, m, bh] = pack(tile[c * CHUNK:(c + 1) * CHUNK])
+                near[c].t[g, m, bh] = pack(tile[STARTS[c]:STARTS[c] + SIZES[c]])
 
     for stream in near:
         stream.over_x()
@@ -181,32 +191,32 @@
 
     arrivals = []
 
-    def far_chunk(c, between):
+    def far_chunk(c):
         exchange[c].wait_recv()
-        rows = pl.ds(c * CHUNK, CHUNK)
+        rows, size = pl.ds(STARTS[c], SIZES[c]), SIZES[c]
 
         @pl.loop(0, 4)
         def _(a):
             left = [held[2 * bh + (a + role + zb) % 2, rows, :] for role in range(2) for bh in range(2)]
             tile = product(jnp.concatenate(left, 0), own[a, :, here])
-            for role in range(2):
-                g, m = group_of(a, role)
-                for bh in range(2):
-                    start = (2 * role + bh) * CHUNK
-                    t[role * AWAY + c, g, m, bh] = pack(tile[start:start + CHUNK])
+            g, m = group_of(a, 0)
+            for bh in range(2):
+                home[c].t[g, m, bh] = pack(tile[bh * size:(bh + 1) * size])
+                going[c].t[bh, (a + 1 + zb) % 2, a // 2] = pack(tile[(2 + bh) * size:(3 + bh) * size])
 
         home[c].over_x()
         going[c].over_x()
-        for stream in between:
-            stream.over_zh()
+        if c == 0:
+            for stream in near:
+                stream.over_zh()
+            exchange[-1].start()
         home[c].over_x_again()
         going[c].over_x_again()
         home[c].over_zh()
-        arrivals.append(going[c].go_home(r5.at[c], homes))
-
-    far_chunk(0, near)
-    far_chunk(1, ())
-    far_chunk(2, ())
+        arrivals.append(going[c].go_home(r5.at[c, :, pl.ds(0, packed_rows(size))], homes))
+
+    for c in range(CHUNKS):
+        far_chunk(c)
 
     for stream in near:
         stream.to_mirror(stream.summed(), near_mirror)
@@ -216,9 +226,11 @@
     for c in range(CHUNKS):
         for copy in arrivals[c]:
             copy.wait_recv()
-    helped = flipped(whole([r5[c, 0] + r5[c, 1] for c in range(CHUNKS)]))
-    for c in range(CHUNKS):
-        home[c].to_mirror(home[c].summed() + pack(helped[c * CHUNK:(c + 1) * CHUNK]), home_mirror)
+    ends = [packed_rows(size) for size in SIZES]
+    helped = flipped(whole([r5[c, 0, :ends[c]] + r5[c, 1, :ends[c]] for c in range(CHUNKS)]))
+    for c in range(CHUNKS):
+        part = helped[STARTS[c]:STARTS[c] + SIZES[c]]
+        home[c].to_mirror(home[c].summed() + pack(part), home_mirror)
     for stream in near:
         stream.copy3.wait_recv()
     out_ref[1, 1 - slot] = whole([stream.r4[...] for stream in near])[:ops, :ops]
@@ -245,7 +257,7 @@
     dma = pltpu.SemaphoreType.DMA
 
     def tiles(*lead):
-        return pltpu.VMEM((*lead, PACKED, 128), jnp.float32)
+        return pltpu.VMEM((*lead, packed_rows(max(SIZES)), 128), jnp.float32)
 
     return pl.pallas_call(
         kernel,

time: 271 us -> 237 us (0.87)
  Pallas kernels: 259 us -> 224 us
    pallas_call x1, Pallas kernels: 259 us -> 224 us  [on_device(): pl.pallas_call(kernel, out_shape=jax.ShapeDtypeStruct((2, 2, ops, ops), j...]
where the time goes in v3:
time: 237 us; the launch traced here: 236 us
  Pallas kernels  224 us (95%)
  local copies, waits for them, and re-layouts  12.3 us (5%)
    pallas_call x1, Pallas kernels, on_device(): pl.pallas_call(kernel, out_shape=jax.ShapeDtypeStruct((2, 2, ops, ops), j...  224 us
    unnamed x1, local copies, waits for them, and re-layouts  5.41 us

profile of v3, /device:TPU:22, one launch (start us, length us, event | category | flops | bytes accessed | tf_op | source)
XLA Modules:
  0.0 236.2 jit_solution(15362989032407714017)
XLA Ops:
  0.0 5.4 %copy.5 = bf16[4,2048,324]{1,2,0:T(8,128)(2,1)S(1)} copy(bf16[4,2048,324]{1,0,2:T(4,128)(2,1)} %param.1) | data formatting | bytes 10616832 | tf_op args[0]
  5.4 3.0 %pad.4.a_ref = bf16[4,328,2048]{2,1,0:T(8,128)(2,1)} pad(bf16[4,324,2048]{2,1,0:T(8,128)(2,1)S(1)} %bitcast.3, bf16[]{:T(256)} %constant.2.clone.1), padding=0_0x0_4x0_0 | pad | bytes 10682370 | tf_op jit(solution)/shard_map/jit(_pad)/pad | solution.py:256
  8.5 223.8 %shard_map.17 = f32[2,2,324,324]{3,2,1,0:T(8,128)} custom-call(bf16[4,328,2048]{2,1,0:T(8,128)(2,1)} %pad.4.a_ref), custom_call_target="tpu_custom_call" | custom-call | tf_op jit(solution)/shard_map/pallas_call | solution.py:262
  232.3 3.9 %copy.3 = f32[2,2,324,324]{3,1,2,0:T(2,128)} copy(f32[2,2,324,324]{3,2,1,0:T(8,128)} %shard_map.17) | data formatting | bytes 3359232 | tf_op jit(solution)/shard_map/pallas_call | solution.py:262

commit v4 on v3

--- a/solution.py
+++ b/solution.py
@@ -65,6 +65,15 @@
         src_ref=source, dst_ref=target, send_sem=sends.at[send_at], recv_sem=recvs.at[recv_at],
         device_id=device, device_id_type=MESH,
     )
+
+
+def by_state(raw, first, target, c):
+    start, size = STARTS[c], SIZES[c]
+
+    @pl.loop(0, target.shape[2] // 256)
+    def _(i):
+        part = pl.ds(pl.multiple_of(i * 256, 256), 256)
+        target[:, start:start + size, part] = jnp.swapaxes(raw[first:first + size, :, part], 0, 1)
 
 
 class Stream:
@@ -130,13 +139,13 @@
 
 
 def kernel(
-    a_ref, out_ref, own, beside, held, t, r1, r2, r3, f, r4, r5,
+    a_ref, out_ref, own, beside, held, raw_own, raw_beside, raw_held, t, r1, r2, r3, f, r4, r5,
     send_sem, recv_sem, load_sem, ex_send, ex_recv,
 ):
     zb, core = lax.axis_index("zb"), lax.axis_index("core")
     x, zh = lax.axis_index("x"), lax.axis_index("zh")
     half = held.shape[2]
-    ops, given = out_ref.shape[2], a_ref.shape[1]
+    ops = out_ref.shape[2]
 
     other = {"zb": 1 - zb}
     home_mirror = {**other, "x": 2 * zh + (x + zb) % 2, "zh": x // 2}
@@ -154,27 +163,38 @@
 
     here = pl.ds(pl.multiple_of(zb * half, half), half)
     away = pl.ds(pl.multiple_of((1 - zb) * half, half), half)
+    valid = [min(size, ops - start) for start, size in zip(STARTS, SIZES)]
     exchange = []
     for c in range(CHUNKS):
-        rows = pl.ds(STARTS[c], min(SIZES[c], given - STARTS[c]))
-        exchange.append(
-            remote(a_ref.at[:, rows, away], held.at[:, rows, :], ex_send, ex_recv, c, c, other)
-        )
+        rows = pl.ds(STARTS[c], valid[c])
+        exchange.append(remote(a_ref.at[rows, :, away], raw_held.at[rows], ex_send, ex_recv, c, c, other))
     for copy in exchange[:-1]:
         copy.start()
-    every = pl.ds(0, given)
-    to_side = remote(a_ref, beside.at[:, every, :], ex_send, ex_recv, CHUNKS, CHUNKS, {"core": 1 - core})
+    to_side = remote(
+        a_ref, raw_beside.at[pl.ds(0, ops)], ex_send, ex_recv, CHUNKS, CHUNKS, {"core": 1 - core}
+    )
     to_side.start()
-    load = pltpu.make_async_copy(a_ref, own.at[:, every, :], load_sem)
-    load.start()
+    loads = [
+        pltpu.make_async_copy(
+            a_ref.at[pl.ds(STARTS[c], valid[c])], raw_own.at[c % 2, pl.ds(0, valid[c])], load_sem.at[c]
+        )
+        for c in range(CHUNKS)
+    ]
+    loads[0].start()
+    for c in range(CHUNKS):
+        if c + 1 < CHUNKS:
+            loads[c + 1].start()
+        loads[c].wait()
+        by_state(raw_own.at[c % 2], 0, own, c)
 
     refs, sems = (t, r1, r2, r3, f, r4), (send_sem, recv_sem)
     home = [Stream(HOME + c, 0, refs, sems) for c in range(CHUNKS)]
     going = [Stream(AWAY + c, 1, refs, sems) for c in range(CHUNKS)]
     near = [Stream(NEAR + c, c % 2, refs, sems) for c in range(CHUNKS)]
 
-    load.wait()
     to_side.wait_recv()
+    for c in range(CHUNKS):
+        by_state(raw_beside, STARTS[c], beside, c)
 
     @pl.loop(0, 4)
     def _(a):
@@ -193,6 +213,7 @@
 
     def far_chunk(c):
         exchange[c].wait_recv()
+        by_state(raw_held, STARTS[c], held, c)
         rows, size = pl.ds(STARTS[c], SIZES[c]), SIZES[c]
 
         @pl.loop(0, 4)
@@ -236,9 +257,10 @@
     out_ref[1, 1 - slot] = whole([stream.r4[...] for stream in near])[:ops, :ops]
     slot = (x + zb) % 2
     out_ref[0, slot] = flipped(whole([stream.f[...] for stream in home]))[:ops, :ops]
-    for stream in home:
-        stream.copy3.wait_recv()
-    out_ref[0, 1 - slot] = whole([stream.r4[...] for stream in home])[:ops, :ops]
+    for c in range(CHUNKS):
+        home[c].copy3.wait_recv()
+        rows = pl.ds(STARTS[c], valid[c])
+        out_ref[0, 1 - slot, rows, :] = unpack(home[c].r4[...], SIZES[c])[:valid[c], :ops]
 
     to_side.wait_send()
     for copy in exchange:
@@ -253,7 +275,6 @@
 
 def on_device(amplitudes):
     states, dets, ops = amplitudes.shape
-    block = jnp.pad(amplitudes.transpose(0, 2, 1), ((0, 0), (0, -ops % 8), (0, 0)))
     dma = pltpu.SemaphoreType.DMA
 
     def tiles(*lead):
@@ -268,6 +289,9 @@
             pltpu.VMEM((states, ROWS, dets), jnp.bfloat16),
             pltpu.VMEM((states, ROWS, dets), jnp.bfloat16),
             pltpu.VMEM((states, ROWS, dets // 2), jnp.bfloat16),
+            pltpu.VMEM((2, max(SIZES), states, dets), jnp.bfloat16),
+            pltpu.VMEM((ROWS, states, dets), jnp.bfloat16),
+            pltpu.VMEM((ROWS, states, dets // 2), jnp.bfloat16),
             tiles(STREAMS, 2, 2, 2),
             tiles(STREAMS, 2, 2),
             tiles(STREAMS, 2),
@@ -277,14 +301,14 @@
             tiles(CHUNKS, 2),
             dma((STREAMS * STEPS,)),
             dma((STREAMS * STEPS,)),
-            dma,
+            dma((CHUNKS,)),
             dma((CHUNKS + 1,)),
             dma((CHUNKS + 1,)),
         ],
         compiler_params=pltpu.CompilerParams(
             collective_id=0, has_side_effects=True, vmem_limit_bytes=64 * 1024 * 1024 - 65536,
         ),
-    )(block)
+    )(amplitudes.transpose(2, 0, 1))
 
 
 def solution(mesh):

time: 237 us -> 229 us (0.966)
  local copies, waits for them, and re-layouts: 12.3 us -> 3.87 us
    unnamed x1 -> x0, local copies, waits for them, and re-layouts: 5.41 us -> none
    pad x1 -> x0, local copies, waits for them, and re-layouts: 3.04 us -> none  [on_device(): jnp.pad(amplitudes.transpose(0, 2, 1), ((0, 0), (0, -ops % 8), (0, 0)))]
where the time goes in v4:
time: 229 us; the launch traced here: 227 us
  Pallas kernels  223 us (97%)
  local copies, waits for them, and re-layouts  3.87 us (2%)
    pallas_call x1, Pallas kernels, on_device(): pl.pallas_call(kernel, out_shape=jax.ShapeDtypeStruct((2, 2, ops, ops), j...  223 us

profile of v4, /device:TPU:22, one launch (start us, length us, event | category | flops | bytes accessed | tf_op | source)
XLA Modules:
  0.0 227.3 jit_solution(16306557618236212615)
XLA Ops:
  0.0 223.5 %shard_map.17 = f32[2,2,324,324]{3,2,1,0:T(8,128)} custom-call(bf16[324,4,2048]{2,1,0:T(4,128)(2,1)} %bitcast.1), custom_call_target="tpu_custom_call" | custom-call | tf_op jit(solution)/shard_map/pallas_call | solution.py:283
  223.5 3.9 %copy.2 = f32[2,2,324,324]{3,1,2,0:T(2,128)} copy(f32[2,2,324,324]{3,2,1,0:T(8,128)} %shard_map.17) | data formatting | bytes 3359232 | tf_op jit(solution)/shard_map/pallas_call | solution.py:283

commit v5 on v4

--- a/solution.py
+++ b/solution.py
@@ -104,13 +104,17 @@
         self.copy1.start()
         self.t[g, m] += self.r1[m]
 
+    def settle(self):
+        self.copy1.wait_recv()
+        for last in range(2):
+            self.t[self.group, self.member, last] += self.r2[last]
+
+    def add(self, last, value):
+        self.t[self.group, self.member, last] += value
+
     def over_zh(self):
-        self.copy1.wait_recv()
-        g, m, h = self.group, self.member, self.zh
-        self.t[g, m, 1 - h] += self.r2[1 - h]
-        self.copy2 = self.copy(2, self.t.at[g, m, 1 - h], self.r3, {"zh": 1 - h})
+        self.copy2 = self.copy(2, self.t.at[self.group, self.member, 1 - self.zh], self.r3, {"zh": 1 - self.zh})
         self.copy2.start()
-        self.t[g, m, h] += self.r2[h]
 
     def summed(self):
         self.copy2.wait_recv()
@@ -121,21 +125,9 @@
         self.copy3 = self.copy(3, self.f, self.r4, device)
         self.copy3.start()
 
-    def go_home(self, r5, homes):
-        self.copy1.wait_recv()
-        g, m = self.group, self.member
-        for bh in range(2):
-            self.t[g, m, bh] += self.r2[bh]
-        self.home_copies = [
-            remote(self.t.at[g, m, bh], r5.at[self.zh], *self.sems, self.sem + 2 + bh, self.sem + 2 + self.zh, homes[bh])
-            for bh in range(2)
-        ]
-        for copy in self.home_copies:
-            copy.start()
-        return [
-            remote(self.t.at[g, m, z], r5.at[z], *self.sems, self.sem + 2 + z, self.sem + 2 + z, homes[z])
-            for z in range(2)
-        ]
+    def across(self, r5, device):
+        self.copy2 = self.copy(2, self.t.at[self.group, self.member], r5, device)
+        self.copy2.start()
 
 
 def kernel(
@@ -150,11 +142,11 @@
     other = {"zb": 1 - zb}
     home_mirror = {**other, "x": 2 * zh + (x + zb) % 2, "zh": x // 2}
     from_mirror = {**other, "x": 2 * zh + (x + 1 - zb) % 2, "zh": x // 2}
-    homes = [{**other, "zh": z} for z in range(2)]
+    joint = {**other, "zh": 1 - zh}
     near_mirror = {"core": 1 - core, "x": 2 * zh + (x + core) % 2, "zh": x // 2}
     partners = [
         {"core": 1 - core}, {"x": x + 1 - 2 * (x % 2)}, {"x": 3 - x}, {"zh": 1 - zh},
-        *homes, home_mirror, from_mirror, near_mirror,
+        other, joint, home_mirror, from_mirror, near_mirror,
     ]
     barrier = pltpu.get_barrier_semaphore()
     for partner in partners:
@@ -168,7 +160,7 @@
     for c in range(CHUNKS):
         rows = pl.ds(STARTS[c], valid[c])
         exchange.append(remote(a_ref.at[rows, :, away], raw_held.at[rows], ex_send, ex_recv, c, c, other))
-    for copy in exchange[:-1]:
+    for copy in exchange:
         copy.start()
     to_side = remote(
         a_ref, raw_beside.at[pl.ds(0, ops)], ex_send, ex_recv, CHUNKS, CHUNKS, {"core": 1 - core}
@@ -209,8 +201,6 @@
     for stream in near:
         stream.over_x_again()
 
-    arrivals = []
-
     def far_chunk(c):
         exchange[c].wait_recv()
         by_state(raw_held, STARTS[c], held, c)
@@ -229,12 +219,13 @@
         going[c].over_x()
         if c == 0:
             for stream in near:
+                stream.settle()
                 stream.over_zh()
-            exchange[-1].start()
         home[c].over_x_again()
         going[c].over_x_again()
-        home[c].over_zh()
-        arrivals.append(going[c].go_home(r5.at[c, :, pl.ds(0, packed_rows(size))], homes))
+        going[c].settle()
+        going[c].across(r5.at[c, :, pl.ds(0, packed_rows(size))], joint)
+        home[c].settle()
 
     for c in range(CHUNKS):
         far_chunk(c)
@@ -244,14 +235,17 @@
     slot = (x + core) % 2
     out_ref[1, slot] = flipped(whole([stream.f[...] for stream in near]))[:ops, :ops]
 
-    for c in range(CHUNKS):
-        for copy in arrivals[c]:
-            copy.wait_recv()
-    ends = [packed_rows(size) for size in SIZES]
-    helped = flipped(whole([r5[c, 0, :ends[c]] + r5[c, 1, :ends[c]] for c in range(CHUNKS)]))
-    for c in range(CHUNKS):
-        part = helped[STARTS[c]:STARTS[c] + SIZES[c]]
-        home[c].to_mirror(home[c].summed() + pack(part), home_mirror)
+    for stream in going:
+        stream.copy2.wait_recv()
+    for last in (1 - zh, zh):
+        helped = flipped(whole([r5[c, last, :packed_rows(SIZES[c])] for c in range(CHUNKS)]))
+        for c in range(CHUNKS):
+            home[c].add(last, pack(helped[STARTS[c]:STARTS[c] + SIZES[c]]))
+        if last is not zh:
+            for stream in home:
+                stream.over_zh()
+    for stream in home:
+        stream.to_mirror(stream.summed(), home_mirror)
     for stream in near:
         stream.copy3.wait_recv()
     out_ref[1, 1 - slot] = whole([stream.r4[...] for stream in near])[:ops, :ops]
@@ -265,12 +259,11 @@
     to_side.wait_send()
     for copy in exchange:
         copy.wait_send()
+    for stream in (*home, *going, *near):
+        for copy in (stream.copy0, stream.copy1, stream.copy2):
+            copy.wait_send()
     for stream in (*home, *near):
-        for copy in (stream.copy0, stream.copy1, stream.copy2, stream.copy3):
-            copy.wait_send()
-    for stream in going:
-        for copy in (stream.copy0, stream.copy1, *stream.home_copies):
-            copy.wait_send()
+        stream.copy3.wait_send()
 
 
 def on_device(amplitudes):

time: 229 us -> 248 us (1.083)
  Pallas kernels: 223 us -> 242 us
    pallas_call x1, Pallas kernels: 223 us -> 242 us  [on_device(): pl.pallas_call(kernel, out_shape=jax.ShapeDtypeStruct((2, 2, ops, ops), j...]
where the time goes in v5:
time: 248 us; the launch traced here: 246 us
  Pallas kernels  242 us (98%)
  local copies, waits for them, and re-layouts  3.87 us (2%)
    pallas_call x1, Pallas kernels, on_device(): pl.pallas_call(kernel, out_shape=jax.ShapeDtypeStruct((2, 2, ops, ops), j...  242 us

profile of v5, /device:TPU:22, one launch (start us, length us, event | category | flops | bytes accessed | tf_op | source)
XLA Modules:
  0.0 246.4 jit_solution(11109272574861958184)
XLA Ops:
  0.0 242.5 %shard_map.17 = f32[2,2,324,324]{3,2,1,0:T(8,128)} custom-call(bf16[324,4,2048]{2,1,0:T(4,128)(2,1)} %bitcast.1), custom_call_target="tpu_custom_call" | custom-call | tf_op jit(solution)/shard_map/pallas_call | solution.py:276
  242.5 3.9 %copy.2 = f32[2,2,324,324]{3,1,2,0:T(2,128)} copy(f32[2,2,324,324]{3,2,1,0:T(8,128)} %shard_map.17) | data formatting | bytes 3359232 | tf_op jit(solution)/shard_map/pallas_call | solution.py:276

commit v6 on v5

--- a/solution.py
+++ b/solution.py
@@ -217,23 +217,32 @@
 
         home[c].over_x()
         going[c].over_x()
+
+    def again(c):
+        home[c].over_x_again()
+        going[c].over_x_again()
+
+    def join(c):
+        going[c].settle()
+        going[c].across(r5.at[c, :, pl.ds(0, packed_rows(SIZES[c]))], joint)
+        home[c].settle()
+
+    for c in range(CHUNKS):
+        far_chunk(c)
         if c == 0:
             for stream in near:
                 stream.settle()
                 stream.over_zh()
-        home[c].over_x_again()
-        going[c].over_x_again()
-        going[c].settle()
-        going[c].across(r5.at[c, :, pl.ds(0, packed_rows(size))], joint)
-        home[c].settle()
-
-    for c in range(CHUNKS):
-        far_chunk(c)
+        if c >= 1:
+            again(c - 1)
+        if c >= 2:
+            join(c - 2)
 
     for stream in near:
         stream.to_mirror(stream.summed(), near_mirror)
-    slot = (x + core) % 2
-    out_ref[1, slot] = flipped(whole([stream.f[...] for stream in near]))[:ops, :ops]
+    again(CHUNKS - 1)
+    join(CHUNKS - 2)
+    join(CHUNKS - 1)
 
     for stream in going:
         stream.copy2.wait_recv()
@@ -244,6 +253,8 @@
         if last is not zh:
             for stream in home:
                 stream.over_zh()
+    slot = (x + core) % 2
+    out_ref[1, slot] = flipped(whole([stream.f[...] for stream in near]))[:ops, :ops]
     for stream in home:
         stream.to_mirror(stream.summed(), home_mirror)
     for stream in near:

time: 248 us -> 254 us (1.024)
  Pallas kernels: 242 us -> 249 us
    pallas_call x1, Pallas kernels: 242 us -> 249 us  [on_device(): pl.pallas_call(kernel, out_shape=jax.ShapeDtypeStruct((2, 2, ops, ops), j...]
where the time goes in v6:
time: 254 us; the launch traced here: 253 us
  Pallas kernels  249 us (98%)
  local copies, waits for them, and re-layouts  3.87 us (2%)
    pallas_call x1, Pallas kernels, on_device(): pl.pallas_call(kernel, out_shape=jax.ShapeDtypeStruct((2, 2, ops, ops), j...  249 us

profile of v6, /device:TPU:22, one launch (start us, length us, event | category | flops | bytes accessed | tf_op | source)
XLA Modules:
  0.0 252.6 jit_solution(18405350073215872875)
XLA Ops:
  0.0 248.8 %shard_map.17 = f32[2,2,324,324]{3,2,1,0:T(8,128)} custom-call(bf16[324,4,2048]{2,1,0:T(4,128)(2,1)} %bitcast.1), custom_call_target="tpu_custom_call" | custom-call | tf_op jit(solution)/shard_map/pallas_call | solution.py:287
  248.8 3.9 %copy.2 = f32[2,2,324,324]{3,1,2,0:T(2,128)} copy(f32[2,2,324,324]{3,2,1,0:T(8,128)} %shard_map.17) | data formatting | bytes 3359232 | tf_op jit(solution)/shard_map/pallas_call | solution.py:287

commit v7 on v6

--- a/solution.py
+++ b/solution.py
@@ -132,9 +132,9 @@
 
 def kernel(
     a_ref, out_ref, own, beside, held, raw_own, raw_beside, raw_held, t, r1, r2, r3, f, r4, r5,
-    send_sem, recv_sem, load_sem, ex_send, ex_recv,
+    send_sem, recv_sem, load_sem, ex_send, ex_recv, credit,
 ):
-    zb, core = lax.axis_index("zb"), lax.axis_index("core")
+    za, zb, core = lax.axis_index("za"), lax.axis_index("zb"), lax.axis_index("core")
     x, zh = lax.axis_index("x"), lax.axis_index("zh")
     half = held.shape[2]
     ops = out_ref.shape[2]
@@ -143,10 +143,11 @@
     home_mirror = {**other, "x": 2 * zh + (x + zb) % 2, "zh": x // 2}
     from_mirror = {**other, "x": 2 * zh + (x + 1 - zb) % 2, "zh": x // 2}
     joint = {**other, "zh": 1 - zh}
+    beyond = {"za": 1 - za, "zb": 1 - zb}
     near_mirror = {"core": 1 - core, "x": 2 * zh + (x + core) % 2, "zh": x // 2}
     partners = [
         {"core": 1 - core}, {"x": x + 1 - 2 * (x % 2)}, {"x": 3 - x}, {"zh": 1 - zh},
-        other, joint, home_mirror, from_mirror, near_mirror,
+        other, joint, beyond, home_mirror, from_mirror, near_mirror,
     ]
     barrier = pltpu.get_barrier_semaphore()
     for partner in partners:
@@ -160,8 +161,23 @@
     for c in range(CHUNKS):
         rows = pl.ds(STARTS[c], valid[c])
         exchange.append(remote(a_ref.at[rows, :, away], raw_held.at[rows], ex_send, ex_recv, c, c, other))
-    for copy in exchange:
-        copy.start()
+    exchange[0].start()
+
+    @pl.when(za == zb)
+    def _():
+        for copy in exchange[1:]:
+            copy.start()
+
+    def arrive(c):
+        exchange[c].wait_recv()
+        if c + 1 < CHUNKS:
+
+            @pl.when(za != zb)
+            def _():
+                pl.semaphore_signal(credit, inc=1, device_id=beyond, device_id_type=MESH)
+                pl.semaphore_wait(credit, 1)
+                exchange[c + 1].start()
+
     to_side = remote(
         a_ref, raw_beside.at[pl.ds(0, ops)], ex_send, ex_recv, CHUNKS, CHUNKS, {"core": 1 - core}
     )
@@ -198,11 +214,13 @@
 
     for stream in near:
         stream.over_x()
+    arrive(0)
     for stream in near:
         stream.over_x_again()
 
     def far_chunk(c):
-        exchange[c].wait_recv()
+        if c > 0:
+            arrive(c)
         by_state(raw_held, STARTS[c], held, c)
         rows, size = pl.ds(STARTS[c], SIZES[c]), SIZES[c]
 
@@ -229,7 +247,7 @@
 
     for c in range(CHUNKS):
         far_chunk(c)
-        if c == 0:
+        if c + 1 == CHUNKS:
             for stream in near:
                 stream.settle()
                 stream.over_zh()
@@ -238,11 +256,11 @@
         if c >= 2:
             join(c - 2)
 
-    for stream in near:
-        stream.to_mirror(stream.summed(), near_mirror)
     again(CHUNKS - 1)
     join(CHUNKS - 2)
     join(CHUNKS - 1)
+    for stream in near:
+        stream.to_mirror(stream.summed(), near_mirror)
 
     for stream in going:
         stream.copy2.wait_recv()
@@ -308,6 +326,7 @@
             dma((CHUNKS,)),
             dma((CHUNKS + 1,)),
             dma((CHUNKS + 1,)),
+            pltpu.SemaphoreType.REGULAR,
         ],
         compiler_params=pltpu.CompilerParams(
             collective_id=0, has_side_effects=True, vmem_limit_bytes=64 * 1024 * 1024 - 65536,

time: 254 us -> 254 us (level)
  no operation moved by 1% of the time
where the time goes in v7:
time: 254 us; the launch traced here: 252 us
  Pallas kernels  248 us (98%)
  local copies, waits for them, and re-layouts  3.87 us (2%)
    pallas_call x1, Pallas kernels, on_device(): pl.pallas_call(kernel, out_shape=jax.ShapeDtypeStruct((2, 2, ops, ops), j...  248 us

profile of v7, /device:TPU:22, one launch (start us, length us, event | category | flops | bytes accessed | tf_op | source)
XLA Modules:
  0.0 252.2 jit_solution(11298159012697913038)
XLA Ops:
  0.0 248.3 %shard_map.17 = f32[2,2,324,324]{3,2,1,0:T(8,128)} custom-call(bf16[324,4,2048]{2,1,0:T(4,128)(2,1)} %bitcast.1), custom_call_target="tpu_custom_call" | custom-call | tf_op jit(solution)/shard_map/pallas_call | solution.py:305
  248.3 3.9 %copy.2 = f32[2,2,324,324]{3,1,2,0:T(2,128)} copy(f32[2,2,324,324]{3,2,1,0:T(8,128)} %shard_map.17) | data formatting | bytes 3359232 | tf_op jit(solution)/shard_map/pallas_call | solution.py:305

commit v8 on v4

--- a/solution.py
+++ b/solution.py
@@ -145,7 +145,7 @@
     zb, core = lax.axis_index("zb"), lax.axis_index("core")
     x, zh = lax.axis_index("x"), lax.axis_index("zh")
     half = held.shape[2]
-    ops = out_ref.shape[2]
+    ops = out_ref.shape[1]
 
     other = {"zb": 1 - zb}
     home_mirror = {**other, "x": 2 * zh + (x + zb) % 2, "zh": x // 2}
@@ -242,7 +242,7 @@
     for stream in near:
         stream.to_mirror(stream.summed(), near_mirror)
     slot = (x + core) % 2
-    out_ref[1, slot] = flipped(whole([stream.f[...] for stream in near]))[:ops, :ops]
+    out_ref[1, :, slot] = flipped(whole([stream.f[...] for stream in near]))[:ops, :ops]
 
     for c in range(CHUNKS):
         for copy in arrivals[c]:
@@ -254,13 +254,13 @@
         home[c].to_mirror(home[c].summed() + pack(part), home_mirror)
     for stream in near:
         stream.copy3.wait_recv()
-    out_ref[1, 1 - slot] = whole([stream.r4[...] for stream in near])[:ops, :ops]
+    out_ref[1, :, 1 - slot] = whole([stream.r4[...] for stream in near])[:ops, :ops]
     slot = (x + zb) % 2
-    out_ref[0, slot] = flipped(whole([stream.f[...] for stream in home]))[:ops, :ops]
+    out_ref[0, :, slot] = flipped(whole([stream.f[...] for stream in home]))[:ops, :ops]
     for c in range(CHUNKS):
         home[c].copy3.wait_recv()
         rows = pl.ds(STARTS[c], valid[c])
-        out_ref[0, 1 - slot, rows, :] = unpack(home[c].r4[...], SIZES[c])[:valid[c], :ops]
+        out_ref[0, rows, 1 - slot] = unpack(home[c].r4[...], SIZES[c])[:valid[c], :ops]
 
     to_side.wait_send()
     for copy in exchange:
@@ -280,9 +280,9 @@
     def tiles(*lead):
         return pltpu.VMEM((*lead, packed_rows(max(SIZES)), 128), jnp.float32)
 
-    return pl.pallas_call(
+    result = pl.pallas_call(
         kernel,
-        out_shape=jax.ShapeDtypeStruct((2, 2, ops, ops), jnp.float32),
+        out_shape=jax.ShapeDtypeStruct((2, ops, 2, ops), jnp.float32),
         in_specs=[pl.BlockSpec(memory_space=pl.ANY)],
         out_specs=pl.BlockSpec(memory_space=pltpu.VMEM),
         scratch_shapes=[
@@ -309,6 +309,7 @@
             collective_id=0, has_side_effects=True, vmem_limit_bytes=64 * 1024 * 1024 - 65536,
         ),
     )(amplitudes.transpose(2, 0, 1))
+    return result.transpose(0, 2, 1, 3)
 
 
 def solution(mesh):

time: 229 us -> 228 us (level)
    pallas_call x1 -> x0, local copies, waits for them, and re-layouts: 3.87 us -> none  [on_device(): pl.pallas_call(kernel, out_shape=jax.ShapeDtypeStruct((2, 2, ops, ops), j...]
    unnamed x0 -> x1, local copies, waits for them, and re-layouts: none -> 3.52 us
where the time goes in v8:
time: 228 us; the launch traced here: 227 us
  Pallas kernels  223 us (98%)
  local copies, waits for them, and re-layouts  3.52 us (2%)
    pallas_call x1, Pallas kernels, on_device(): pl.pallas_call(kernel, out_shape=jax.ShapeDtypeStruct((2, ops, 2, ops), j...  223 us

profile of v8, /device:TPU:22, one launch (start us, length us, event | category | flops | bytes accessed | tf_op | source)
XLA Modules:
  0.0 227.0 jit_solution(13165362934521486180)
XLA Ops:
  0.0 223.4 %shard_map.17 = f32[2,324,2,324]{3,2,1,0:T(2,128)} custom-call(bf16[324,4,2048]{2,1,0:T(4,128)(2,1)} %bitcast.3), custom_call_target="tpu_custom_call" | custom-call | tf_op jit(solution)/shard_map/pallas_call | solution.py:283
  223.5 3.5 %copy.3 = f32[2,2,324,324]{3,1,2,0:T(2,128)} copy(f32[2,2,324,324]{3,1,2,0:T(2,128)} %bitcast.2) | data formatting | bytes 3359232

commit v9 on v8

--- a/solution.py
+++ b/solution.py
@@ -10,6 +10,7 @@
 LANES = 384
 SIZES = (96, 96, 80, 64)
 STARTS = (0, 96, 192, 272)
+KEPT = (96, 96, 80, 56)
 CHUNKS = len(SIZES)
 HOME, AWAY, NEAR = 0, CHUNKS, 2 * CHUNKS
 STREAMS = 3 * CHUNKS
@@ -30,15 +31,23 @@
     return lax.broadcasted_iota(jnp.int32, (rows, 128), 1)
 
 
+def folded_rows(size):
+    return (size + 15) // 16 * 8
+
+
 def packed_rows(size):
-    return 2 * size + size // 2 + 8
+    return 2 * size + folded_rows(size) + 8
 
 
 def pack(tile):
     size, third = tile.shape[0], tile[:, 256:]
     if third.shape[1] < 128:
         third = jnp.concatenate([third, jnp.zeros((size, 128 - third.shape[1]), jnp.float32)], 1)
-    folded = jnp.where(lanes(size // 2) < 64, third[:size // 2], pltpu.roll(third[size // 2:], 64, 1))
+    fold = folded_rows(size)
+    lower = third[fold:]
+    if lower.shape[0] < fold:
+        lower = jnp.concatenate([lower, jnp.zeros((fold - lower.shape[0], 128), jnp.float32)], 0)
+    folded = jnp.where(lanes(fold) < 64, third[:fold], pltpu.roll(lower, 64, 1))
     rest = jnp.concatenate([third, jnp.zeros((128 - size, 128), jnp.float32)], 0).T[64:72]
     return jnp.concatenate([tile[:, :128], tile[:, 128:256], folded, rest], 0)
 
@@ -46,18 +55,18 @@
 def unpack(packed, size):
     end = packed_rows(size)
     folded = packed[2 * size:end - 8]
-    third = jnp.concatenate([folded, pltpu.roll(folded, 64, 1)], 0)
+    third = jnp.concatenate([folded, pltpu.roll(folded, 64, 1)[:size - folded.shape[0]]], 0)
     rest = jnp.concatenate([packed[end - 8:], jnp.zeros((120, 128), jnp.float32)], 0).T[:size]
     third = jnp.where(lanes(size) < 64, third, pltpu.roll(rest, 64, 1))
     return jnp.concatenate([packed[:size], packed[size:2 * size], third], 1)
 
 
 def whole(chunks):
-    return jnp.concatenate([unpack(chunk, size) for chunk, size in zip(chunks, SIZES)], 0)
+    return jnp.concatenate([unpack(chunk, size) for chunk, size in zip(chunks, KEPT)], 0)
 
 
 def flipped(tile):
-    return jnp.concatenate([tile, jnp.zeros((LANES - ROWS, LANES), jnp.float32)], 0).T
+    return jnp.concatenate([tile, jnp.zeros((LANES - tile.shape[0], LANES), jnp.float32)], 0).T
 
 
 def remote(source, target, sends, recvs, send_at, recv_at, device):
@@ -78,7 +87,7 @@
 
 class Stream:
     def __init__(self, index, scheme, refs, sems):
-        rows = pl.ds(0, packed_rows(SIZES[index % CHUNKS]))
+        rows = pl.ds(0, packed_rows(KEPT[index % CHUNKS]))
         t, r1, r2, r3, f, r4 = refs
         self.t, self.r1 = t.at[index, :, :, :, rows], r1.at[index, :, :, rows]
         self.r2 = r2.at[index, :, rows]
@@ -168,7 +177,7 @@
     for c in range(CHUNKS):
         rows = pl.ds(STARTS[c], valid[c])
         exchange.append(remote(a_ref.at[rows, :, away], raw_held.at[rows], ex_send, ex_recv, c, c, other))
-    for copy in exchange[:-1]:
+    for copy in exchange:
         copy.start()
     to_side = remote(
         a_ref, raw_beside.at[pl.ds(0, ops)], ex_send, ex_recv, CHUNKS, CHUNKS, {"core": 1 - core}
@@ -202,7 +211,7 @@
             tile = product(beside[2 * bh + (a + core) % 2], own[a])
             for c in range(CHUNKS):
                 g, m = group_of(a, c % 2)
-                near[c].t[g, m, bh] = pack(tile[STARTS[c]:STARTS[c] + SIZES[c]])
+                near[c].t[g, m, bh] = pack(tile[STARTS[c]:STARTS[c] + KEPT[c]])
 
     for stream in near:
         stream.over_x()
@@ -222,22 +231,32 @@
             tile = product(jnp.concatenate(left, 0), own[a, :, here])
             g, m = group_of(a, 0)
             for bh in range(2):
-                home[c].t[g, m, bh] = pack(tile[bh * size:(bh + 1) * size])
-                going[c].t[bh, (a + 1 + zb) % 2, a // 2] = pack(tile[(2 + bh) * size:(3 + bh) * size])
+                home[c].t[g, m, bh] = pack(tile[bh * size:bh * size + KEPT[c]])
+                going[c].t[bh, (a + 1 + zb) % 2, a // 2] = pack(tile[(2 + bh) * size:(2 + bh) * size + KEPT[c]])
 
         home[c].over_x()
         going[c].over_x()
-        if c == 0:
+
+    def again(c):
+        home[c].over_x_again()
+        going[c].over_x_again()
+
+    def join(c):
+        home[c].over_zh()
+        arrivals.append(going[c].go_home(r5.at[c, :, pl.ds(0, packed_rows(KEPT[c]))], homes))
+
+    for c in range(CHUNKS):
+        far_chunk(c)
+        if c + 1 == CHUNKS:
             for stream in near:
                 stream.over_zh()
-            exchange[-1].start()
-        home[c].over_x_again()
-        going[c].over_x_again()
-        home[c].over_zh()
-        arrivals.append(going[c].go_home(r5.at[c, :, pl.ds(0, packed_rows(size))], homes))
-
-    for c in range(CHUNKS):
-        far_chunk(c)
+        if c >= 1:
+            again(c - 1)
+        if c >= 2:
+            join(c - 2)
+    again(CHUNKS - 1)
+    join(CHUNKS - 2)
+    join(CHUNKS - 1)
 
     for stream in near:
         stream.to_mirror(stream.summed(), near_mirror)
@@ -247,10 +266,10 @@
     for c in range(CHUNKS):
         for copy in arrivals[c]:
             copy.wait_recv()
-    ends = [packed_rows(size) for size in SIZES]
+    ends = [packed_rows(size) for size in KEPT]
     helped = flipped(whole([r5[c, 0, :ends[c]] + r5[c, 1, :ends[c]] for c in range(CHUNKS)]))
     for c in range(CHUNKS):
-        part = helped[STARTS[c]:STARTS[c] + SIZES[c]]
+        part = helped[STARTS[c]:STARTS[c] + KEPT[c]]
         home[c].to_mirror(home[c].summed() + pack(part), home_mirror)
     for stream in near:
         stream.copy3.wait_recv()
@@ -260,7 +279,7 @@
     for c in range(CHUNKS):
         home[c].copy3.wait_recv()
         rows = pl.ds(STARTS[c], valid[c])
-        out_ref[0, rows, 1 - slot] = unpack(home[c].r4[...], SIZES[c])[:valid[c], :ops]
+        out_ref[0, rows, 1 - slot] = unpack(home[c].r4[...], KEPT[c])[:valid[c], :ops]
 
     to_side.wait_send()
     for copy in exchange:
@@ -278,7 +297,7 @@
     dma = pltpu.SemaphoreType.DMA
 
     def tiles(*lead):
-        return pltpu.VMEM((*lead, packed_rows(max(SIZES)), 128), jnp.float32)
+        return pltpu.VMEM((*lead, packed_rows(max(KEPT)), 128), jnp.float32)
 
     result = pl.pallas_call(
         kernel,

time: 228 us -> 226 us (level)
    pallas_call x1, Pallas kernels: 223 us -> 221 us  [on_device(): pl.pallas_call(kernel, out_shape=jax.ShapeDtypeStruct((2, ops, 2, ops), j...]
where the time goes in v9:
time: 226 us; the launch traced here: 225 us
  Pallas kernels  221 us (98%)
  local copies, waits for them, and re-layouts  3.52 us (2%)
    pallas_call x1, Pallas kernels, on_device(): pl.pallas_call(kernel, out_shape=jax.ShapeDtypeStruct((2, ops, 2, ops), j...  221 us

profile of v9, /device:TPU:22, one launch (start us, length us, event | category | flops | bytes accessed | tf_op | source)
XLA Modules:
  0.0 224.6 jit_solution(11398549531174694062)
XLA Ops:
  0.0 221.1 %shard_map.17 = f32[2,324,2,324]{3,2,1,0:T(2,128)} custom-call(bf16[324,4,2048]{2,1,0:T(4,128)(2,1)} %bitcast.3), custom_call_target="tpu_custom_call" | custom-call | tf_op jit(solution)/shard_map/pallas_call | solution.py:302
  221.1 3.5 %copy.3 = f32[2,2,324,324]{3,1,2,0:T(2,128)} copy(f32[2,2,324,324]{3,1,2,0:T(2,128)} %bitcast.2) | data formatting | bytes 3359232

commit v10 on v9

--- a/solution.py
+++ b/solution.py
@@ -8,9 +8,9 @@
 MESH = pl.DeviceIdType.MESH
 ROWS = 336
 LANES = 384
-SIZES = (96, 96, 80, 64)
-STARTS = (0, 96, 192, 272)
-KEPT = (96, 96, 80, 56)
+SIZES = (112, 96, 80, 48)
+STARTS = (0, 112, 208, 288)
+KEPT = (112, 96, 80, 40)
 CHUNKS = len(SIZES)
 HOME, AWAY, NEAR = 0, CHUNKS, 2 * CHUNKS
 STREAMS = 3 * CHUNKS

time: 226 us -> 231 us (1.022)
  the two profiles are of different devices: /device:TPU:22 before, /device:TPU:1 now
where the time goes in v10:
time: 231 us
  Pallas kernels  227 us (98%)
  local copies, waits for them, and re-layouts  3.52 us (2%)
    pallas_call x1, Pallas kernels, on_device(): pl.pallas_call(kernel, out_shape=jax.ShapeDtypeStruct((2, ops, 2, ops), j...  227 us

profile of v10, /device:TPU:1, one launch (start us, length us, event | category | flops | bytes accessed | tf_op | source)
XLA Modules:
  0.0 230.8 jit_solution(11649358987202560204)
XLA Ops:
  0.0 227.2 %shard_map.17 = f32[2,324,2,324]{3,2,1,0:T(2,128)} custom-call(bf16[324,4,2048]{2,1,0:T(4,128)(2,1)} %bitcast.3), custom_call_target="tpu_custom_call" | custom-call | tf_op jit(solution)/shard_map/pallas_call | solution.py:302
  227.2 3.5 %copy.3 = f32[2,2,324,324]{3,1,2,0:T(2,128)} copy(f32[2,2,324,324]{3,1,2,0:T(2,128)} %bitcast.2) | data formatting | bytes 3359232
